TPU v7x, 512 devices: a whole 4x4x16 slice. The times are simulated.
512 devices in a mesh: cls: 8 (over z_lo, core), ptcl: 64 (over y, z_hi, x).
Axes of the slice: x: 4, y: 4, z: 16 (z_hi: 4, z_lo: 4; z = z_hi * 4 + z_lo), core: 2. Of those that a mesh axis runs over, the one named last changes fastest.
Arguments:
- particles: bfloat16 [65536, 2048], P('ptcl')
- panels: bfloat16 [8, 128, 2048], P('cls', 'ptcl')
- sigma2: float32 [32], replicated, may hold values from 0.5 to 2
- defocus_bins: int32 [65536], P('ptcl'), may hold values from 0 to 15
- half_sets: int32 [65536], P('ptcl'), may hold values 0 or 1
- prior_mask: int32 [65536, 8], P('ptcl', 'cls'), may hold values from 0 to 1, as said below
- orient_ids: int32 [128], replicated, may hold values from 0 to 127, each once
Outputs:
- half_maps: float32 [8, 256, 2048], P('cls', 'ptcl')
- log_evidence: float32 [65536], P('ptcl')
Inputs may be any that keep to these rules, and one draw needn't show every extreme that they name: `prior_mask`: every particle allows at least one class. `orient_ids`: each direction 0 to 127 appears once.
All inputs are finite; a program needn't handle non-finite values. No bound on the sum of `half_sets` on one device may be relied on, other than what follows from the above.
Results may differ from a plain program's by a relative error of at most 0.0015.
The roundings to bfloat16 on the way count: a program that leaves them out, or rounds other values in their place, can miss the bound.
Values may be sent and summed in bfloat16 or wider, within the bound.
No kernel may reach another device: no remote copies, remote signals or barrier semaphores. Data moves between devices by JAX's collectives and lax.ppermute only.
A program may use at most 64 MiB of HBM per device.

v0:
```python
import jax
import jax.numpy as jnp
from jax import lax
from jax.sharding import PartitionSpec as P

PIXC = 1024
ORIENT = 128
NSHELL = 32
NBIN = 16


def from_partner(shard, axis, apart):
    return lax.ppermute(shard, axis, [(i, i ^ 1 << apart) for i in range(lax.axis_size(axis))])


def ctf_table():
    bins = jnp.arange(NBIN, dtype=jnp.float32)
    defocus = (bins + 1.0) / NBIN
    radius = (jnp.arange(PIXC, dtype=jnp.float32) + 0.5) / PIXC
    phase = 0.3 + 2.5 * defocus[:, None] * radius[None, :]
    return jnp.sin(phase) + 0.1 * jnp.cos(phase)


def lookup_small(indices, values):
    count = values.shape[0]
    match = indices[:, None] == jnp.arange(count, dtype=jnp.int32)[None, :]
    return jnp.sum(jnp.where(match, values[None, :], 0.0), axis=1)


def contract_rows(left, right):
    return lax.dot_general(
        left, right, (((0,), (0,)), ((), ())), preferred_element_type=jnp.float32
    )


def on_device(particles, panels, sigma2, defocus_bins, half_sets, prior_mask, orient_ids):
    shells = jnp.arange(PIXC, dtype=jnp.int32) * NSHELL // PIXC
    inverse_noise = lookup_small(shells, 1.0 / sigma2)
    table = ctf_table()
    onehot_bin = (defocus_bins[:, None] == jnp.arange(NBIN, dtype=jnp.int32)[None, :]).astype(
        jnp.float32
    )
    contrast = jnp.dot(onehot_bin, table, precision=lax.Precision.HIGHEST)
    doubled = jnp.concatenate([contrast, contrast], axis=1)
    noise_pair = jnp.concatenate([inverse_noise, inverse_noise])
    images = particles.astype(jnp.float32)
    weighted = (images * doubled * noise_pair[None, :]).astype(jnp.bfloat16)
    power = (contrast * contrast * inverse_noise[None, :]).astype(jnp.bfloat16)
    piece = lax.all_gather(panels[0], "ptcl", axis=0, tiled=True)
    piece_f = piece.astype(jnp.float32)
    piece_power = (piece_f[:, :PIXC] ** 2 + piece_f[:, PIXC:] ** 2).astype(jnp.bfloat16)
    direct = lax.dot_general(
        weighted, piece, (((1,), (1,)), ((), ())), preferred_element_type=jnp.float32
    )
    norm_part = lax.dot_general(
        power, piece_power, (((1,), (1,)), ((), ())), preferred_element_type=jnp.float32
    )
    scores = direct - 0.5 * norm_part
    allowed = (prior_mask[:, 0] > 0)[:, None]
    masked = jnp.where(allowed, scores, -1e30)
    local_peak = jnp.max(masked, axis=1)
    peak = lax.pmax(local_peak, "cls")
    weights_exp = jnp.where(allowed, jnp.exp(masked - peak[:, None]), 0.0)
    total = lax.psum(jnp.sum(weights_exp, axis=1), "cls")
    log_evidence = peak + jnp.log(total)
    posterior = (weights_exp / total[:, None]).astype(jnp.bfloat16)
    permuter = (orient_ids[:, None] == jnp.arange(ORIENT, dtype=jnp.int32)[None, :]).astype(
        jnp.bfloat16
    )
    by_direction = jnp.dot(posterior, permuter, preferred_element_type=jnp.float32).astype(
        jnp.bfloat16
    )
    half_col = half_sets.astype(jnp.bfloat16)[:, None]
    split_post = jnp.concatenate([by_direction * (1 - half_col), by_direction * half_col], axis=1)
    centred = (images * doubled).astype(jnp.bfloat16)
    squares_ctf = (contrast * contrast).astype(jnp.bfloat16)
    stacked = jnp.concatenate([centred, squares_ctf], axis=1)
    summed = lax.psum_scatter(
        contract_rows(split_post, stacked), "ptcl", scatter_dimension=0, tiled=True
    )
    data = summed[:, : 2 * PIXC]
    weight = summed[:, 2 * PIXC :]
    top_bit = lax.axis_size("ptcl").bit_length() - 2
    partner = from_partner(data.astype(jnp.bfloat16), "ptcl", top_bit).astype(data.dtype)
    half_index = lax.axis_index("ptcl") // (lax.axis_size("ptcl") // 2)

    def per_shell(values):
        summed_rows = jnp.sum(values, axis=0)
        folded = summed_rows[:PIXC] + summed_rows[PIXC:]
        return jnp.sum(folded.reshape(NSHELL, PIXC // NSHELL), axis=1)

    cross = per_shell(data * partner)
    own_power = per_shell(data * data)
    is_first = half_index == 0
    stats = jnp.stack(
        [0.5 * cross, jnp.where(is_first, own_power, 0.0), jnp.where(is_first, 0.0, own_power)]
    )
    totals = lax.psum(stats, "ptcl")
    fsc = totals[0] / jnp.sqrt(totals[1] * totals[2] + 1e-06)
    factor = (1.0 + lookup_small(shells, fsc)) / 2.0
    factor_pair = jnp.concatenate([factor, factor])
    weight_pair = jnp.concatenate([weight, weight], axis=1)
    half_maps = data * factor_pair[None, :] / (weight_pair + 1.0)
    return (half_maps[None], log_evidence)


def solution(mesh):
    placed = (
        P("ptcl", None),
        P("cls", "ptcl", None),
        P(),
        P("ptcl"),
        P("ptcl"),
        P("ptcl", "cls"),
        P(),
    )
    return jax.shard_map(
        on_device,
        mesh=mesh,
        in_specs=placed,
        out_specs=(P("cls", "ptcl", None), P("ptcl")),
        check_vma=False,
    )
```

profile of v0, /device:TPU:32, one launch (start us, length us, event | category | flops | bytes accessed | tf_op | source)
XLA Modules:
  0.0 1377.2 jit_solution(9083316655074497782)
XLA Ops:
  7.2 0.0 all-reduce.3.cloned.1.call-start
  7.3 0.7 broadcast_divide_fusion
  7.9 0.1 select_reduce_fusion.1
  8.0 0.0 copy-start.2
  8.0 6.4 copy.14
  14.5 234.2 %all-gather = bf16[1,128,2048]{2,0,1:T(2,128)(2,1)S(1)} all-gather(bf16[1,2,2048]{2,0,1:T(2,128)(2,1)S(1)} %copy.15), channel_id=2, replica_groups=mesh['cls'=8,'ptcl'=64] {'ptcl'}, dimensions={1}, use_global_device_ids=true | all-gather | bytes 532480 | tf_op jit(solution)/shard_map/all_gather | solution.py:49
  248.7 0.4 bitcast_convert_fusion
  249.1 2.2 multiply_convert_fusion.3
  251.3 3.3 fusion
  254.6 1.5 fusion.5
  256.2 0.7 fusion.46
  256.9 10.0 pmax.7
  266.9 0.1 fusion.18
  267.0 13.5 psum.14
  280.5 0.3 broadcast_multiply_fusion.1
  280.9 5.8 fusion.1
  286.7 0.0 all-reduce.3.cloned.1.call-update
  286.7 1.3 dynamic-slice
  288.6 848.2 %all-reduce.3.cloned.1.call-done = f32[256,3072]{1,0:T(8,128)} async-done(((f32[256,3072]{1,0:T(8,128)}), f32[256,3072]{1,0:T(8,128)}) %all-reduce.3.cloned.1.call-update) | async-done | bytes 3145744
  1136.8 0.8 dynamic-slice_convert_fusion
  1137.6 1.9 collective-permute-start
  1139.5 0.6 log_add_fusion
  1140.2 0.8 dynamic-slice.3
  1141.0 3.8 collective-permute-done
  1144.8 0.9 multiply_reduce_fusion.1
  1145.7 0.1 add.87
  1145.7 0.1 add.85
  1145.8 0.1 reduce_sum.68
  1145.9 0.1 reduce_sum.66
  1146.1 222.7 %psum.15 = f32[3,32]{1,0:T(4,128)S(1)} all-reduce(f32[3,32]{1,0:T(4,128)S(1)} %pad_maximum_fusion.2), channel_id=1, replica_groups=mesh['cls'=8,'ptcl'=64] {'ptcl'}, use_global_device_ids=true, to_apply=%region_10.11 | all-reduce | flops 96 | bytes 768 | tf_op jit(solution)/shard_map/psum | solution.py:98
  1368.8 0.1 select_reduce_fusion
  1368.9 1.5 fusion.35
  (25 shorter events, 0.1 us)
Async XLA Ops:
  7.2 1129.6 %all-reduce.3.cloned.1.call-start = ((), (), s32[]{:S(2)}) async-start(), calls=%async_computation | async-start | bytes 6291456
  8.0 6.4 copy-start.1
  8.0 241.0 %copy-start.2 = (s32[1024]{0:T(1024)S(1)}, s32[1024]{0:T(1024)}, u32[]{:S(2)}) copy-start(s32[1024]{0:T(1024)} %param.10) | copy-start | bytes 12292
  248.7 2.6 copy-start
  254.6 1.5 copy-start.3
  256.1 24.4 %copy-start.4 = (s32[1024]{0:T(1024)S(1)}, s32[1024]{0:T(1024)}, u32[]{:S(2)}) copy-start(s32[1024]{0:T(1024)} %param.11) | copy-start | bytes 12292
  256.1 24.4 %copy-start.5 = (s32[128]{0:T(128)S(1)}, s32[128]{0:T(128)}, u32[]{:S(2)}) copy-start(s32[128]{0:T(128)} %param.13) | copy-start | bytes 1540
  1137.6 7.1 collective-permute-start
Sparse Core Ops, SparseCore 0:
  286.8 849.9 all-reduce.2
where the time goes:
time: 1380 us
  waiting for transfers between devices  852 us (62%)
  blocking collectives  480 us (35%)
  between operations  14.9 us (1%)
    unnamed x2, waiting for transfers between devices  848 us
    all_gather x1, blocking collectives, on_device(): piece = lax.all_gather(panels[0], 'ptcl', axis=0, tiled=True)  234 us
    psum x1, blocking collectives, on_device(): totals = lax.psum(stats, 'ptcl')  223 us
  transfers between devices with their start and end apart: 2, of which 2 were waited for; matrix products, arithmetic and copies ran while one was open for 0% of the time, Pallas kernels for 0%

commit v1 on v0

--- a/solution.py
+++ b/solution.py
@@ -46,7 +46,10 @@
     images = particles.astype(jnp.float32)
     weighted = (images * doubled * noise_pair[None, :]).astype(jnp.bfloat16)
     power = (contrast * contrast * inverse_noise[None, :]).astype(jnp.bfloat16)
-    piece = lax.all_gather(panels[0], "ptcl", axis=0, tiled=True)
+    piece = jnp.concatenate(
+        jax.lax.all_to_all(jnp.stack([panels[0]] * jax.lax.psum(1, "ptcl"), axis=0), "ptcl", 0, 0),
+        0,
+    )
     piece_f = piece.astype(jnp.float32)
     piece_power = (piece_f[:, :PIXC] ** 2 + piece_f[:, PIXC:] ** 2).astype(jnp.bfloat16)
     direct = lax.dot_general(

time: 1380 us -> 1200 us (0.87)
  blocking collectives: 480 us -> 244 us
  waiting for transfers between devices: 852 us -> 879 us
  starting transfers between devices: 1.96 us -> 22.3 us
    all_gather x1 -> x0, blocking collectives: 234 us -> none  [on_device(): piece = lax.all_gather(panels[0], 'ptcl', axis=0, tiled=True)]
    all_to_all x0 -> x1, waiting for transfers between devices: none -> 22.2 us  [on_device(): jax.lax.all_to_all(jnp.stack([panels[0]] * jax.lax.psum(1, 'ptcl'), axis=...]
    all_to_all x0 -> x1, starting transfers between devices: none -> 20.3 us  [on_device(): jax.lax.all_to_all(jnp.stack([panels[0]] * jax.lax.psum(1, 'ptcl'), axis=...]
  transfers between devices with their start and end apart: 2 -> 3, of which waited for: 2 -> 3; matrix products, arithmetic and copies ran while one was open for 0% -> 1% of each run, Pallas kernels for 0% -> 0%
where the time goes in v1:
time: 1200 us
  waiting for transfers between devices  879 us (73%)
  blocking collectives  244 us (20%)
  starting transfers between devices  22.3 us (2%)
  between operations  14.9 us (1%)
  matrix products  14.5 us (1%)
  local copies, waits for them, and re-layouts  13.8 us (1%)
    unnamed x2, waiting for transfers between devices  853 us
    psum x1, blocking collectives, on_device(): totals = lax.psum(stats, 'ptcl')  223 us
  transfers between devices with their start and end apart: 3, of which 3 were waited for; matrix products, arithmetic and copies ran while one was open for 1% of the time, Pallas kernels for 0%

profile of v1, /device:TPU:32, one launch (start us, length us, event | category | flops | bytes accessed | tf_op | source)
XLA Modules:
  0.0 1195.9 jit_solution(12878862586434508725)
XLA Ops:
  7.2 1.8 stack.4
  9.0 20.3 %all-to-all-start = ((bf16[64,2,2048]{2,1,0:T(2,128)(2,1)}), bf16[64,2,2048]{2,1,0:T(2,128)(2,1)S(1)}, u32[]{:S(2)}, u32[]{:S(2)}) async-start(bf16[64,2,2048]{2,1,0:T(2,128)(2,1)} %stack.4), calls=%async_computation | async-start | bytes 1048576 | tf_op jit(solution)/shard_map/all_to_all | solution.py:50
  29.4 6.4 copy.11
  35.8 0.1 select_reduce_fusion.1
  36.0 2.2 multiply_convert_fusion.3
  38.3 2.0 copy-done
  40.2 3.2 fusion
  43.5 22.2 %all-to-all-done = bf16[64,2,2048]{2,1,0:T(2,128)(2,1)S(1)} async-done(((bf16[64,2,2048]{2,1,0:T(2,128)(2,1)}), bf16[64,2,2048]{2,1,0:T(2,128)(2,1)S(1)}, u32[]{:S(2)}, u32[]{:S(2)}) %all-to-all-start) | async-done | bytes 524320 | tf_op jit(solution)/shard_map/all_to_all | solution.py:50
  65.7 0.2 reshape.114
  65.9 0.1 convert_element_type.41
  66.0 5.5 fusion.5
  71.5 0.3 copy-done.1
  71.8 0.7 fusion.44
  72.6 10.6 pmax.7
  83.2 0.1 fusion.17
  83.3 10.8 psum.14
  94.1 0.3 broadcast_multiply_fusion.1
  94.4 5.7 fusion.1
  100.2 1.3 dynamic-slice
  102.1 853.3 %all-reduce.3.cloned.1.call-done = f32[256,3072]{1,0:T(8,128)} async-done(((f32[256,3072]{1,0:T(8,128)}), f32[256,3072]{1,0:T(8,128)}) %all-reduce.3.cloned.1.call-update) | async-done | bytes 3145744
  955.4 0.8 dynamic-slice_convert_fusion
  956.3 1.9 collective-permute-start
  958.2 0.6 log_add_fusion
  958.8 0.8 dynamic-slice.3
  959.6 3.8 collective-permute-done
  963.4 0.9 multiply_reduce_fusion.1
  964.3 0.1 add.87
  964.4 0.1 reduce_sum.68
  964.6 0.1 reduce_sum.66
  964.7 222.7 %psum.15 = f32[3,32]{1,0:T(4,128)S(1)} all-reduce(f32[3,32]{1,0:T(4,128)S(1)} %pad_maximum_fusion.2), channel_id=1, replica_groups=mesh['cls'=8,'ptcl'=64] {'ptcl'}, use_global_device_ids=true, to_apply=%region_10.11 | all-reduce | flops 96 | bytes 768 | tf_op jit(solution)/shard_map/psum | solution.py:101
  1187.4 0.1 select_reduce_fusion
  1187.5 1.5 fusion.33
  (31 shorter events, 0.3 us)
Async XLA Ops:
  9.0 56.7 %all-to-all-start = ((bf16[64,2,2048]{2,1,0:T(2,128)(2,1)}), bf16[64,2,2048]{2,1,0:T(2,128)(2,1)S(1)}, u32[]{:S(2)}, u32[]{:S(2)}) async-start(bf16[64,2,2048]{2,1,0:T(2,128)(2,1)} %stack.4), calls=%async_computation | async-start | bytes 1048576 | tf_op jit(solution)/shard_map/all_to_all | solution.py:50
  29.3 926.1 %all-reduce.3.cloned.1.call-start = ((), (), s32[]{:S(2)}) async-start(), calls=%async_computation.1 | async-start | bytes 6291456
  29.3 6.5 copy-start.6
  29.3 6.6 copy-start.4
  29.3 6.6 copy-start.5
  29.4 6.6 copy-start.3
  35.8 4.4 copy-start.2
  38.2 2.0 copy-start
  66.0 5.8 copy-start.1
  71.8 22.2 %copy-start.7 = (s32[128]{0:T(128)S(1)}, s32[128]{0:T(128)}, u32[]{:S(2)}) copy-start(s32[128]{0:T(128)} %param.13) | copy-start | bytes 1540
  956.3 7.1 collective-permute-start
Sparse Core Ops, SparseCore 0:
  100.3 855.0 all-reduce.2
